TPU v7x, 256 devices: a whole 4x4x8 slice. The times are simulated.
256 devices in a mesh: band: 8 (over x, core), col: 32 (over z, y).
Axes of the slice: x: 4, y: 4, z: 8, core: 2. Of those that a mesh axis runs over, the one named last changes fastest.
Arguments:
- fields_in: float32 [6, 137, 32, 4096], P(None, None, 'band', 'col'), may hold values from -6 to 6
- drag_rate: float32 [137], replicated, may hold values from 0.1 to 1
- loss_rate: float32 [4, 137], replicated, may hold values from 0.1 to 1
- diffusivity: float32 [6, 136], replicated, may hold values from 0.1 to 10
- owner_col: int32 [8, 16384, 1], P('band', 'col'), may hold values from 0 to 31; in each aligned block of 512 rows (0 to 511, 512 to 1023, ..., all dimensions but the last counted through in order) at most 32 rows name the same one
- anchor_cell: int32 [8, 16384], P('band', 'col'), may hold values from 0 to 124
- offsets: float32 [2, 8, 16384], P(None, 'band', 'col'), may hold values from 0 to 1
- stencil: float32 [4, 32, 4096], P(None, 'band', 'col'), may hold values from 0.02 to 0.24
Outputs:
- fields_out: float32 [6, 137, 32, 4096], P(None, None, 'band', 'col')
Inputs may be any that keep to these rules, and one draw needn't show every extreme that they name: `owner_col`: among the columns of one device at most 32 have the same owner; on some device one owner has exactly 32 of them. The stencil lies inside the owner's block: row anchor_cell // 125, longitude anchor_cell % 125.
All inputs are finite; a program needn't handle non-finite values.
Results may differ from a plain program's by a relative error of at most 0.00002.
Values sent between devices are 32-bit elements; how exact they have to be, the bound alone decides.
No kernel may reach another device: no remote copies, remote signals or barrier semaphores. Data moves between devices by JAX's collectives and lax.ppermute only.
A program may use at most 128 MiB of HBM per device.

v0:
```python
import jax
import jax.numpy as jnp
from jax import lax
from jax.experimental import pallas as pl
from jax.experimental.pallas import tpu as pltpu
from jax.sharding import PartitionSpec as P

F32 = jnp.float32
BF16 = jnp.bfloat16
HI = lax.Precision.HIGHEST
FIELDS = 6
LEV = 137
ROWS = 4
LON = 128
CELLS = 512
PEERS = 32
CAP = 32
LANES = 128
GROUPS = LANES // CAP
FLAT = FIELDS * LEV
CHUNK = 208
PADDED = GROUPS * CHUNK
LEV_PAD = 256


def iota(shape, dim):
    return lax.broadcasted_iota(jnp.int32, shape, dim)


def dot_nn(a, b, precision=None):
    return lax.dot_general(
        a, b, (((1,), (0,)), ((), ())), precision=precision, preferred_element_type=F32
    )


def dot_nt(a, b, precision=None):
    return lax.dot_general(
        a, b, (((1,), (1,)), ((), ())), precision=precision, preferred_element_type=F32
    )


def cubic_weights(frac):
    return (
        -frac * (frac - 1.0) * (frac - 2.0) / 6.0,
        (frac + 1.0) * (frac - 1.0) * (frac - 2.0) / 2.0,
        -(frac + 1.0) * frac * (frac - 2.0) / 2.0,
        (frac + 1.0) * frac * (frac - 1.0) / 6.0,
    )


def split_2(x):
    high = x.astype(BF16)
    return high, (x - high.astype(F32)).astype(BF16)


def group_transpose(parts):
    group = iota(parts[0].shape, 1) // CAP

    def pick(choices):
        out = choices[0]
        for n in range(1, GROUPS):
            out = jnp.where(group == n, choices[n], out)
        return out

    turned = []
    for shift in range(GROUPS):
        mixed = pick([parts[(n + shift) % GROUPS] for n in range(GROUPS)])
        turned.append(pltpu.roll(mixed, shift * CAP, 1) if shift else mixed)
    return [pick([turned[(n - b) % GROUPS] for n in range(GROUPS)]) for b in range(GROUPS)]


def request_kernel(owner_ref, anchor_ref, offsets_ref, req_ref, slot_ref):
    owner = owner_ref[...]
    onehot = (iota((PEERS, CELLS), 0) == owner).astype(F32)
    earlier = (iota((CELLS, CELLS), 0) < iota((CELLS, CELLS), 1)).astype(BF16)
    before = dot_nn(onehot.astype(BF16), earlier)
    position = jnp.sum(onehot * before, axis=0, keepdims=True).astype(jnp.int32)
    slot_ref[...] = owner * CAP + position
    total = jnp.zeros((PEERS, LANES), F32)
    lane = iota((LANES, CELLS), 0)
    rows = (anchor_ref[...].astype(F32), offsets_ref[0:1, :], offsets_ref[1:2, :])
    for part, row in enumerate(rows):
        place = (lane == part * CAP + position).astype(F32)
        total = total + dot_nt(onehot * row, place, HI)
    req_ref[...] = total


def source_kernel(x_ref, drag_ref, loss_ref, diff_ref, y_ref, z_ref, rate_s, k_s, b0_s, b1_s, x_s):
    rate_s[...] = jnp.zeros_like(rate_s)
    k_s[...] = jnp.zeros_like(k_s)
    rate_s[0:1, 0:LEV] = drag_ref[...]
    rate_s[1:5, 0:LEV] = loss_ref[...]
    k_s[0:FIELDS, 0 : LEV - 1] = diff_ref[...]
    rates = jnp.transpose(rate_s[...])
    diff = k_s[...]
    lane = iota((8, LEV_PAD), 1)
    lane_half = iota((8, LANES), 1)
    top = jnp.ones((8, LANES), F32)
    low = jnp.ones((8, LANES), F32)
    tops = [jnp.ones((8, LANES), F32)] * 2
    lows = [jnp.ones((8, LANES), F32)] * 2
    for level in range(LEV):
        if level % 12 == 11:
            low = low / top
            top = jnp.ones((8, LANES), F32)
        k = jnp.broadcast_to(diff[:, level : level + 1], (8, LANES))
        both = top + k * low
        half_at = level // LANES
        here = lane_half == level % LANES
        lows[half_at] = jnp.where(here, low, lows[half_at])
        tops[half_at] = jnp.where(here, both, tops[half_at])
        top, low = both + k * top, both
    inv = jnp.concatenate(lows, axis=1) / jnp.concatenate(tops, axis=1)
    ratio = diff * inv
    for side in (b0_s, b1_s):
        side[LEV * 8 :, :] = jnp.zeros((LEV_PAD * 8 - LEV * 8, LANES), F32)
    line = jnp.zeros((8, LEV_PAD), F32)
    for level in range(LEV - 1, -1, -1):
        factor = jnp.broadcast_to(ratio[:, level : level + 1], (8, LEV_PAD))
        line = factor * line + (lane == level).astype(F32)
        b0_s[level * 8 : level * 8 + 8, :] = line[:, :LANES]
        b1_s[level * 8 : level * 8 + 8, :] = line[:, LANES:]
    x_s[:, LEV - 1 :, :] = jnp.zeros((FIELDS, LEV_PAD - LEV + 1, 2 * CELLS), F32)
    for row in range(ROWS):
        cells = slice(row * LON, row * LON + LON)
        halves = slice(CELLS + row * LON, CELLS + row * LON + LON)

        def load(field):
            return x_ref[pl.ds(field * LEV * ROWS + row, LEV, stride=ROWS), :]

        u, v = load(0), load(1)
        speed = jnp.sqrt(u * u + v * v + 1.0)
        drag = -0.5 * rates[0:LEV, 0:1] * speed
        for field in range(FIELDS):
            if field < 2:
                value = (u, v)[field]
                half = drag * value
            else:
                value = load(field)
                half = -0.5 * rates[0:LEV, field - 1 : field] * value
            x_s[field, 0:LEV, cells] = value + half
            x_s[field, 0:LEV, halves] = half
    y_ref[FLAT - 6 :, :] = jnp.zeros((PADDED - FLAT + 6, CELLS), F32)
    z_ref[FLAT - 6 :, :] = jnp.zeros((PADDED - FLAT + 6, CELLS), F32)
    for field in range(FIELDS):
        upper = jnp.concatenate(
            [side[pl.ds(field, LEV_PAD, stride=8), :] for side in (b0_s, b1_s)], axis=1
        )
        inverse = dot_nt(upper * inv[field : field + 1, :], upper, HI)
        result = dot_nn(inverse, x_s[field], HI)
        y_ref[field * LEV : field * LEV + LEV, :] = result[0:LEV, 0:CELLS]
        z_ref[field * LEV : field * LEV + LEV, :] = result[0:LEV, CELLS:]


def owner_kernel(got_ref, y_ref, out_ref):
    got = got_ref[...]
    group = iota((PEERS, LANES), 1) // CAP
    mine = iota((PEERS, LANES), 0) % GROUPS == group
    turned = [got] + [pltpu.roll(got, n * CAP, 1) for n in range(1, GROUPS)]
    params = []
    for part in range(3):
        out = turned[(0 - part) % GROUPS]
        for n in range(1, GROUPS):
            out = jnp.where(group == n, turned[(n - part) % GROUPS], out)
        params.append(jnp.where(mine, out, 0.0))
    y_high, y_low = split_2(y_ref[...])
    place = iota((LON, LANES), 0)

    def weights(tile):
        start, lon, lat = (
            jnp.sum(part[tile * GROUPS : (tile + 1) * GROUPS, :], axis=0, keepdims=True)
            for part in params
        )
        offset = place - start.astype(jnp.int32)
        lon_weights = cubic_weights(lon)
        lat_weights = cubic_weights(lat)
        cubic = jnp.zeros((LON, LANES), F32)
        for n in range(4):
            cubic = jnp.where(offset == n, lon_weights[n], cubic)
        linear = jnp.where(offset == 1, 1.0 - lon, jnp.where(offset == 2, lon, 0.0))
        return jnp.concatenate(
            [
                lat_weights[0] * linear,
                lat_weights[1] * cubic,
                lat_weights[2] * cubic,
                lat_weights[3] * linear,
            ],
            axis=0,
        )

    for pair in range(PEERS // GROUPS // 2):
        matrix = jnp.concatenate([weights(2 * pair), weights(2 * pair + 1)], axis=1)
        m_high, m_low = split_2(matrix)
        values = dot_nn(y_high, m_high) + dot_nn(y_high, m_low) + dot_nn(y_low, m_high)
        for side in range(2):
            lanes = slice(side * LANES, side * LANES + LANES)
            parts = [values[g * CHUNK : (g + 1) * CHUNK, lanes] for g in range(GROUPS)]
            for n, block in enumerate(group_transpose(parts)):
                out_ref[(2 * pair + side) * GROUPS + n] = block


def arrive_kernel(got_ref, slot_ref, z_ref, solved_ref, top_ref, bottom_ref, west_ref, east_ref, r_s):
    for tile in range(PEERS // GROUPS):
        lanes = slice(tile * LANES, tile * LANES + LANES)
        parts = [got_ref[tile * GROUPS + n] for n in range(GROUPS)]
        for g, block in enumerate(group_transpose(parts)):
            rows = slice(g * CHUNK, (g + 1) * CHUNK)
            for piece in range(3):
                short = block.astype(BF16)
                r_s[piece, rows, lanes] = short
                block = block - short.astype(F32)
    slots = PEERS * CAP
    pick = (iota((slots, CELLS), 0) == slot_ref[...]).astype(BF16)
    solved = z_ref[...]
    solved = solved + (dot_nn(r_s[2], pick) + dot_nn(r_s[1], pick) + dot_nn(r_s[0], pick))
    solved_ref[...] = solved
    top_ref[...] = solved[:, 0:LON]
    bottom_ref[...] = solved[:, CELLS - LON :]
    row = iota((8, CELLS), 0)
    spot = iota((8, CELLS), 1)
    edge = (spot == (row % ROWS) * LON + (row // ROWS) * (LON - 1)).astype(F32)
    edges = dot_nt(edge, solved, HI)
    west_ref[...] = edges[0:ROWS]
    east_ref[...] = edges[ROWS:]


def stencil_kernel(solved_ref, north_ref, south_ref, west_ref, east_ref, stencil_ref, out_ref):
    sides = jnp.transpose(jnp.concatenate([west_ref[...], east_ref[...]], axis=0))
    lane = iota((PADDED, LON), 1)
    rows = [solved_ref[:, r * LON : (r + 1) * LON] for r in range(ROWS)]
    for r in range(ROWS):
        here = rows[r]
        north = north_ref[...] if r == 0 else rows[r - 1]
        south = south_ref[...] if r == ROWS - 1 else rows[r + 1]
        west = jnp.where(lane == 0, sides[:, r : r + 1], pltpu.roll(here, 1, 1))
        east = jnp.where(
            lane == LON - 1, sides[:, ROWS + r : ROWS + r + 1], pltpu.roll(here, LON - 1, 1)
        )
        result = here
        for n, side in enumerate((north, south, west, east)):
            result = result + stencil_ref[n * ROWS + r : n * ROWS + r + 1, :] * (side - here)
        out_ref[pl.ds(r, FLAT, stride=ROWS), :] = result[0:FLAT]


def shape_of(*dims, dtype=F32):
    return jax.ShapeDtypeStruct(dims, dtype)


def shift(cells, axis, step):
    count = lax.axis_size(axis)
    pairs = [(i, i + step) for i in range(count) if 0 <= i + step < count]
    return lax.ppermute(cells, axis, pairs)


def on_device(
    fields_in, drag_rate, loss_rate, diffusivity, owner_col, anchor_cell, offsets, stencil
):
    flat_in = fields_in.reshape(FLAT * ROWS, LON)
    request, slot_index = pl.pallas_call(
        request_kernel,
        out_shape=(shape_of(PEERS, LANES), shape_of(1, CELLS, dtype=jnp.int32)),
        name="request",
    )(owner_col.reshape(1, CELLS), anchor_cell.reshape(1, CELLS), offsets.reshape(2, CELLS))
    got = lax.all_to_all(request, "col", split_axis=0, concat_axis=0, tiled=True)
    source, local = pl.pallas_call(
        source_kernel,
        out_shape=(shape_of(PADDED, CELLS), shape_of(PADDED, CELLS)),
        scratch_shapes=[
            pltpu.VMEM((8, LEV_PAD), F32),
            pltpu.VMEM((8, LEV_PAD), F32),
            pltpu.VMEM((LEV_PAD * 8, LANES), F32),
            pltpu.VMEM((LEV_PAD * 8, LANES), F32),
            pltpu.VMEM((FIELDS, LEV_PAD, 2 * CELLS), F32),
        ],
        name="source",
    )(flat_in, drag_rate.reshape(1, LEV), loss_rate, diffusivity)
    values = pl.pallas_call(
        owner_kernel, out_shape=shape_of(PEERS, CHUNK, LANES), name="owner"
    )(got, source)
    returned = lax.all_to_all(values, "col", split_axis=0, concat_axis=0, tiled=True)
    solved, top, bottom, west, east = pl.pallas_call(
        arrive_kernel,
        out_shape=(
            shape_of(PADDED, CELLS),
            shape_of(PADDED, LON),
            shape_of(PADDED, LON),
            shape_of(ROWS, PADDED),
            shape_of(ROWS, PADDED),
        ),
        scratch_shapes=[pltpu.VMEM((3, PADDED, PEERS * CAP), BF16)],
        name="arrive",
    )(returned, slot_index, local)
    from_north = shift(bottom, "band", 1)
    from_south = shift(top, "band", -1)
    from_west = shift(east, "col", 1)
    from_east = shift(west, "col", -1)
    out = pl.pallas_call(
        stencil_kernel, out_shape=shape_of(FLAT * ROWS, LON), name="stencil"
    )(solved, from_north, from_south, from_west, from_east, stencil.reshape(4 * ROWS, LON))
    return out.reshape(fields_in.shape)


def solution(mesh):
    in_specs = (
        P(None, None, "band", "col"),
        P(),
        P(),
        P(),
        P("band", "col", None),
        P("band", "col"),
        P(None, "band", "col"),
        P(None, "band", "col"),
    )
    out_specs = P(None, None, "band", "col")
    return jax.shard_map(
        on_device, mesh=mesh, in_specs=in_specs, out_specs=out_specs, check_vma=False
    )
```

profile of v0, /device:TPU:26, one launch (start us, length us, event | category | flops | bytes accessed | tf_op | source)
XLA Modules:
  0.0 157.9 jit_solution(3808103690150182707)
XLA Ops:
  0.0 1.3 copy.12
  1.3 2.4 %request.1 = (f32[32,128]{1,0:T(8,128)}, s32[1,512]{1,0:T(1,128)}) custom-call(s32[1,512]{1,0:T(1,128)} %bitcast.17, s32[1,512]{1,0:T(1,128)} %anchor_ref.1, f32[2,512]{1,0:T(2,128)} %bitcast.15), custom_call_target="tpu_custom_call" | custom-call | tf_op jit(solution)/shard_map/request/pallas_call | solution.py:259
  3.7 11.5 %all-to-all-start = ((f32[32,1,128]{2,1,0:T(1,128)}), f32[32,1,128]{2,1,0:T(1,128)S(1)}, u32[]{:S(2)}, u32[]{:S(2)}) async-start(f32[32,1,128]{2,1,0:T(1,128)} %bitcast.14), calls=%async_computation | async-start | bytes 32768 | tf_op jit(solution)/shard_map/all_to_all | solution.py:264
  15.2 12.2 %source.1 = (f32[832,512]{1,0:T(8,128)}, f32[832,512]{1,0:T(8,128)}) custom-call(f32[3288,128]{1,0:T(8,128)} %bitcast.12, f32[1,137]{1,0:T(1,128)} %bitcast.18, f32[4,137]{1,0:T(4,128)} %loss_ref.1, f32[6,136]{1,0:T(8,128)} %diff_ref.1), custom_call_target="tpu_custom_call" | custom-call | tf_op jit(solution)/shard_map/source/pallas_call | solution.py:265
  27.4 0.0 all-to-all-done
  27.4 0.6 copy-done.2
  28.0 8.8 %owner.1 = f32[32,208,128]{2,1,0:T(8,128)} custom-call(f32[32,128]{1,0:T(8,128)} %bitcast.13, f32[832,512]{1,0:T(8,128)} %get-tuple-element.15.y_ref), custom_call_target="tpu_custom_call" | custom-call | tf_op jit(solution)/shard_map/owner/pallas_call | solution.py:277
  36.8 88.0 %all_to_all.16.got_ref = f32[32,208,128]{2,1,0:T(8,128)} all-to-all(f32[32,208,128]{2,1,0:T(8,128)} %owner.1), channel_id=1, replica_groups=mesh['band'=8,'col'=32] {'col'}, dimensions={0} | all-to-all | bytes 6815744 | tf_op jit(solution)/shard_map/all_to_all | solution.py:280
  124.7 9.6 %arrive.1 = (f32[832,512]{1,0:T(8,128)}, f32[832,128]{1,0:T(8,128)}, f32[832,128]{1,0:T(8,128)}, f32[4,832]{1,0:T(4,128)}, f32[4,832]{1,0:T(4,128)}) custom-call(f32[32,208,128]{2,1,0:T(8,128)} %all_to_all.16.got_ref, s32[1,512]{1,0:T(1,128)} %get-tuple-element.16.slot_ref, f32[832,512]{1,0:T(8,128)} %get-tuple-element.17.z_ref), custom_call_target="tpu_custom_call" | custom-call | tf_op jit(solution)/shard_map/arrive/pallas_call | solution.py:281
  134.3 1.9 %collective-permute-start = (f32[832,128]{1,0:T(8,128)}, f32[832,128]{1,0:T(8,128)S(1)}, u32[]{:S(2)}, u32[]{:S(2)}) collective-permute-start(f32[832,128]{1,0:T(8,128)} %get-tuple-element.19), channel_id=1, source_target_pairs={{0,32},{32,64},{64,96},{96,128},{128,160},{160,192},{192,224},{1,3... | collective-permute-start | bytes 1277960 | tf_op jit(solution)/shard_map/ppermute | solution.py:252
  136.2 3.6 %collective-permute-start.1 = (f32[832,128]{1,0:T(8,128)}, f32[832,128]{1,0:T(8,128)S(1)}, u32[]{:S(2)}, u32[]{:S(2)}) collective-permute-start(f32[832,128]{1,0:T(8,128)} %get-tuple-element.20), channel_id=1, source_target_pairs={{32,0},{64,32},{96,64},{128,96},{160,128},{192,160},{224,192},{33,... | collective-permute-start | bytes 1277960 | tf_op jit(solution)/shard_map/ppermute | solution.py:252
  139.9 4.2 %collective-permute-start.2 = (f32[4,832]{1,0:T(4,128)}, f32[4,832]{1,0:T(4,128)S(1)}, u32[]{:S(2)}, u32[]{:S(2)}) collective-permute-start(f32[4,832]{1,0:T(4,128)} %get-tuple-element.21), channel_id=1, source_target_pairs={{0,1},{1,2},{2,3},{3,4},{4,5},{5,6},{6,7},{7,8},{8,9},{9,10},{10,1... | collective-permute-start | bytes 39944 | tf_op jit(solution)/shard_map/ppermute | solution.py:252
  144.1 1.9 %collective-permute-start.3 = (f32[4,832]{1,0:T(4,128)}, f32[4,832]{1,0:T(4,128)S(1)}, u32[]{:S(2)}, u32[]{:S(2)}) collective-permute-start(f32[4,832]{1,0:T(4,128)} %get-tuple-element.22), channel_id=1, source_target_pairs={{1,0},{2,1},{3,2},{4,3},{5,4},{6,5},{7,6},{8,7},{9,8},{10,9},{11,1... | collective-permute-start | bytes 39944 | tf_op jit(solution)/shard_map/ppermute | solution.py:252
  146.0 0.0 collective-permute-done.2.west_ref
  146.0 0.0 copy-start.3
  146.1 6.0 %collective-permute-done.3.east_ref = f32[4,832]{1,0:T(4,128)S(1)} collective-permute-done((f32[4,832]{1,0:T(4,128)}, f32[4,832]{1,0:T(4,128)S(1)}, u32[]{:S(2)}, u32[]{:S(2)}) %collective-permute-start.3) | collective-permute-done | bytes 13344 | tf_op jit(solution)/shard_map/ppermute | solution.py:252
  152.0 0.0 collective-permute-done.north_ref
  152.0 0.0 collective-permute-done.1.south_ref
  152.0 0.0 copy-start.1
  152.1 0.0 copy-done.3
  152.1 0.6 copy-done.4
  152.6 0.2 copy-done
  152.8 0.2 copy-done.1
  153.0 4.9 %stencil.1 = f32[3288,128]{1,0:T(8,128)} custom-call(f32[832,512]{1,0:T(8,128)} %get-tuple-element.18.solved_ref, f32[832,128]{1,0:T(8,128)} %copy-done, f32[832,128]{1,0:T(8,128)} %copy-done.1, f32[4,832]{1,0:T(4,128)} %copy-done.3, f32[4,832]{1,0:T(4,128)} %copy-done.4, f32[16,128]{1,0:T(8,128)} %bitcast.16), custom_call_target="tpu_custom_call" | custom-call | tf_op jit(solution)/shard_map/stencil/pallas_call | solution.py:297
  (3 shorter events, 0.0 us)
Async XLA Ops:
  3.7 23.7 %all-to-all-start = ((f32[32,1,128]{2,1,0:T(1,128)}), f32[32,1,128]{2,1,0:T(1,128)S(1)}, u32[]{:S(2)}, u32[]{:S(2)}) async-start(f32[32,1,128]{2,1,0:T(1,128)} %bitcast.14), calls=%async_computation | async-start | bytes 32768 | tf_op jit(solution)/shard_map/all_to_all | solution.py:264
  27.4 0.6 copy-start.2
  134.3 17.7 %collective-permute-start = (f32[832,128]{1,0:T(8,128)}, f32[832,128]{1,0:T(8,128)S(1)}, u32[]{:S(2)}, u32[]{:S(2)}) collective-permute-start(f32[832,128]{1,0:T(8,128)} %get-tuple-element.19), channel_id=1, source_target_pairs={{0,32},{32,64},{64,96},{96,128},{128,160},{160,192},{192,224},{1,3... | collective-permute-start | bytes 1277960 | tf_op jit(solution)/shard_map/ppermute | solution.py:252
  136.2 15.8 %collective-permute-start.1 = (f32[832,128]{1,0:T(8,128)}, f32[832,128]{1,0:T(8,128)S(1)}, u32[]{:S(2)}, u32[]{:S(2)}) collective-permute-start(f32[832,128]{1,0:T(8,128)} %get-tuple-element.20), channel_id=1, source_target_pairs={{32,0},{64,32},{96,64},{128,96},{160,128},{192,160},{224,192},{33,... | collective-permute-start | bytes 1277960 | tf_op jit(solution)/shard_map/ppermute | solution.py:252
  139.9 6.2 %collective-permute-start.2 = (f32[4,832]{1,0:T(4,128)}, f32[4,832]{1,0:T(4,128)S(1)}, u32[]{:S(2)}, u32[]{:S(2)}) collective-permute-start(f32[4,832]{1,0:T(4,128)} %get-tuple-element.21), channel_id=1, source_target_pairs={{0,1},{1,2},{2,3},{3,4},{4,5},{5,6},{6,7},{7,8},{8,9},{9,10},{10,1... | collective-permute-start | bytes 39944 | tf_op jit(solution)/shard_map/ppermute | solution.py:252
  144.1 7.9 %collective-permute-start.3 = (f32[4,832]{1,0:T(4,128)}, f32[4,832]{1,0:T(4,128)S(1)}, u32[]{:S(2)}, u32[]{:S(2)}) collective-permute-start(f32[4,832]{1,0:T(4,128)} %get-tuple-element.22), channel_id=1, source_target_pairs={{1,0},{2,1},{3,2},{4,3},{5,4},{6,5},{7,6},{8,7},{9,8},{10,9},{11,1... | collective-permute-start | bytes 39944 | tf_op jit(solution)/shard_map/ppermute | solution.py:252
  146.0 6.0 %copy-start.3 = (f32[4,832]{1,0:T(4,128)}, f32[4,832]{1,0:T(4,128)S(1)}, u32[]{:S(2)}) copy-start(f32[4,832]{1,0:T(4,128)S(1)} %collective-permute-done.2.west_ref) | copy-start | bytes 39940
  152.0 0.6 copy-start.4
  152.0 0.8 copy-start
  152.0 0.9 copy-start.1
where the time goes:
time: 158 us
  blocking collectives  88 us (56%)
  Pallas kernels  37.9 us (24%)
  starting transfers between devices  23.2 us (15%)
  waiting for transfers between devices  5.99 us (4%)
  local copies, waits for them, and re-layouts  2.78 us (2%)
    all_to_all x1, blocking collectives, on_device(): lax.all_to_all(values, 'col', split_axis=0, concat_axis=0, tiled=True)  88 us
    pallas_call x1, Pallas kernels, on_device(): pl.pallas_call(source_kernel, out_shape=(shape_of(PADDED, CELLS), shape_o...  12.2 us
    ppermute x4, starting transfers between devices, shift(): return lax.ppermute(cells, axis, pairs)  11.7 us
    all_to_all x1, starting transfers between devices, on_device(): lax.all_to_all(request, 'col', split_axis=0, concat_axis=0, tiled=True)  11.5 us
    pallas_call x1, Pallas kernels, on_device(): pl.pallas_call(arrive_kernel, out_shape=(shape_of(PADDED, CELLS), shape_o...  9.57 us
    pallas_call x1, Pallas kernels, on_device(): pl.pallas_call(owner_kernel, out_shape=shape_of(PEERS, CHUNK, LANES), nam...  8.77 us
    ppermute x4, waiting for transfers between devices, shift(): return lax.ppermute(cells, axis, pairs)  5.99 us
    pallas_call x1, Pallas kernels, on_device(): pl.pallas_call(stencil_kernel, out_shape=shape_of(FLAT * ROWS, LON), name...  4.89 us
  transfers between devices with their start and end apart: 5, of which 1 were waited for; matrix products, arithmetic and copies ran while one was open for 0% of the time, Pallas kernels for 8%

commit v1 on v0

v1 whole, which is shorter than its diff:
```python
from functools import partial

import jax
import jax.numpy as jnp
from jax import lax
from jax.experimental import pallas as pl
from jax.experimental.pallas import tpu as pltpu
from jax.sharding import PartitionSpec as P

F32 = jnp.float32
BF16 = jnp.bfloat16
HI = lax.Precision.HIGHEST
FIELDS = 6
LEV = 137
ROWS = 4
LON = 128
CELLS = 512
PEERS = 32
CAP = 32
LANES = 128
GROUPS = LANES // CAP
FLAT = FIELDS * LEV
CHUNK = 208
PADDED = GROUPS * CHUNK
SHARES = (208,)
STARTS = tuple(GROUPS * sum(SHARES[:n]) for n in range(len(SHARES)))
COUNTS = tuple(GROUPS * share for share in SHARES)
LEV_PAD = 256
LEV_ROWS = 144


def iota(shape, dim):
    return lax.broadcasted_iota(jnp.int32, shape, dim)


def dot_nn(a, b, precision=None):
    return lax.dot_general(
        a, b, (((1,), (0,)), ((), ())), precision=precision, preferred_element_type=F32
    )


def dot_nt(a, b, precision=None):
    return lax.dot_general(
        a, b, (((1,), (1,)), ((), ())), precision=precision, preferred_element_type=F32
    )


def cubic_weights(frac):
    return (
        -frac * (frac - 1.0) * (frac - 2.0) / 6.0,
        (frac + 1.0) * (frac - 1.0) * (frac - 2.0) / 2.0,
        -(frac + 1.0) * frac * (frac - 2.0) / 2.0,
        (frac + 1.0) * frac * (frac - 1.0) / 6.0,
    )


def split_2(x):
    high = x.astype(BF16)
    return high, (x - high.astype(F32)).astype(BF16)


def dot_split(a, b):
    a_high, a_low = split_2(a)
    b_high, b_low = split_2(b)
    return dot_nn(a_high, b_high) + dot_nn(a_high, b_low) + dot_nn(a_low, b_high)


def store_shares(refs, start, value):
    for ref, low, count in zip(refs, STARTS, COUNTS):
        first, last = max(low, start), min(low + count, start + value.shape[0])
        if first < last:
            ref[first - low : last - low, :] = value[first - start : last - start]


def half_steps(x_ref, rates, row):
    def load(field):
        return x_ref[pl.ds(field * LEV * ROWS + row, LEV, stride=ROWS), :]

    u, v = load(0), load(1)
    drag = -0.5 * rates[0:LEV, 0:1] * jnp.sqrt(u * u + v * v + 1.0)
    for field in range(FIELDS):
        value = (u, v)[field] if field < 2 else load(field)
        rate = drag if field < 2 else -0.5 * rates[0:LEV, field - 1 : field]
        yield field, value, rate * value


def solve_kernel(x_ref, rate_ref, inverse_ref, *refs, moved):
    out_refs, x_s = refs[:-1], refs[-1]
    rates = rate_ref[...]
    x_s[:, LEV - 1 :, :] = jnp.zeros((FIELDS, LEV_PAD - LEV + 1, CELLS), F32)
    for row in range(ROWS):
        for field, value, half in half_steps(x_ref, rates, row):
            x_s[field, 0:LEV, row * LON : row * LON + LON] = value + half if moved else half
    store_shares(out_refs, FLAT, jnp.zeros((PADDED - FLAT, CELLS), F32))
    for field in range(FIELDS):
        result = dot_split(inverse_ref[field], x_s[field])
        store_shares(out_refs, field * LEV, result[0:LEV])


def group_transpose(parts):
    group = iota(parts[0].shape, 1) // CAP

    def pick(choices):
        out = choices[0]
        for n in range(1, GROUPS):
            out = jnp.where(group == n, choices[n], out)
        return out

    turned = []
    for shift in range(GROUPS):
        mixed = pick([parts[(n + shift) % GROUPS] for n in range(GROUPS)])
        turned.append(pltpu.roll(mixed, shift * CAP, 1) if shift else mixed)
    return [pick([turned[(n - b) % GROUPS] for n in range(GROUPS)]) for b in range(GROUPS)]


def request_kernel(owner_ref, anchor_ref, offsets_ref, req_ref, slot_ref):
    owner = owner_ref[...]
    onehot = (iota((PEERS, CELLS), 0) == owner).astype(F32)
    earlier = (iota((CELLS, CELLS), 0) < iota((CELLS, CELLS), 1)).astype(BF16)
    before = dot_nn(onehot.astype(BF16), earlier)
    position = jnp.sum(onehot * before, axis=0, keepdims=True).astype(jnp.int32)
    slot_ref[...] = owner * CAP + position
    total = jnp.zeros((PEERS, LANES), F32)
    lane = iota((LANES, CELLS), 0)
    rows = (anchor_ref[...].astype(F32), offsets_ref[0], offsets_ref[1])
    for part, row in enumerate(rows):
        place = (lane == part * CAP + position).astype(F32)
        total = total + dot_nt(onehot * row, place, HI)
    req_ref[...] = total


def inverse_kernel(drag_ref, loss_ref, diff_ref, rate_ref, inverse_ref, rate_s, k_s, b0_s, b1_s):
    rate_s[...] = jnp.zeros_like(rate_s)
    k_s[...] = jnp.zeros_like(k_s)
    rate_s[0:1, 0:LEV] = drag_ref[...]
    rate_s[1:5, 0:LEV] = loss_ref[...]
    k_s[0:FIELDS, 0 : LEV - 1] = diff_ref[...]
    rate_ref[...] = jnp.transpose(rate_s[...])
    diff = k_s[...]
    lane = iota((8, LEV_PAD), 1)
    lane_half = iota((8, LANES), 1)
    top = jnp.ones((8, LANES), F32)
    low = jnp.ones((8, LANES), F32)
    tops = [jnp.ones((8, LANES), F32)] * 2
    lows = [jnp.ones((8, LANES), F32)] * 2
    for level in range(LEV):
        if level % 12 == 11:
            low = low / top
            top = jnp.ones((8, LANES), F32)
        k = jnp.broadcast_to(diff[:, level : level + 1], (8, LANES))
        both = top + k * low
        half_at = level // LANES
        here = lane_half == level % LANES
        lows[half_at] = jnp.where(here, low, lows[half_at])
        tops[half_at] = jnp.where(here, both, tops[half_at])
        top, low = both + k * top, both
    inv = jnp.concatenate(lows, axis=1) / jnp.concatenate(tops, axis=1)
    ratio = diff * inv
    for side in (b0_s, b1_s):
        side[LEV * 8 :, :] = jnp.zeros((LEV_PAD * 8 - LEV * 8, LANES), F32)
    line = jnp.zeros((8, LEV_PAD), F32)
    for level in range(LEV - 1, -1, -1):
        factor = jnp.broadcast_to(ratio[:, level : level + 1], (8, LEV_PAD))
        line = factor * line + (lane == level).astype(F32)
        b0_s[level * 8 : level * 8 + 8, :] = line[:, :LANES]
        b1_s[level * 8 : level * 8 + 8, :] = line[:, LANES:]
    for field in range(FIELDS):
        upper = jnp.concatenate(
            [side[pl.ds(field, LEV_PAD, stride=8), :] for side in (b0_s, b1_s)], axis=1
        )
        inverse_ref[field] = dot_nt(upper * inv[field : field + 1, :], upper, HI)[0:LEV_ROWS]


def owner_kernel(got_ref, y_ref, out_ref, high_s, low_s):
    share = out_ref.shape[1]

    @pl.when(pl.program_id(0) == 0)
    def _():
        high_s[...], low_s[...] = split_2(y_ref[...])

    got = got_ref[...]
    group = iota(got.shape, 1) // CAP
    mine = iota(got.shape, 0) % GROUPS == group
    turned = [got] + [pltpu.roll(got, n * CAP, 1) for n in range(1, GROUPS)]
    params = []
    for part in range(3):
        out = turned[(0 - part) % GROUPS]
        for n in range(1, GROUPS):
            out = jnp.where(group == n, turned[(n - part) % GROUPS], out)
        params.append(jnp.where(mine, out, 0.0))
    place = iota((LON, LANES), 0)

    def weights(tile):
        start, lon, lat = (
            jnp.sum(part[tile * GROUPS : (tile + 1) * GROUPS, :], axis=0, keepdims=True)
            for part in params
        )
        offset = place - start.astype(jnp.int32)
        lon_weights = cubic_weights(lon)
        lat_weights = cubic_weights(lat)
        cubic = jnp.zeros((LON, LANES), F32)
        for n in range(4):
            cubic = jnp.where(offset == n, lon_weights[n], cubic)
        linear = jnp.where(offset == 1, 1.0 - lon, jnp.where(offset == 2, lon, 0.0))
        return jnp.concatenate(
            [
                lat_weights[0] * linear,
                lat_weights[1] * cubic,
                lat_weights[2] * cubic,
                lat_weights[3] * linear,
            ],
            axis=0,
        )

    matrix = jnp.concatenate([weights(0), weights(1)], axis=1)
    m_high, m_low = split_2(matrix)
    values = dot_nn(high_s[...], m_high) + dot_nn(high_s[...], m_low) + dot_nn(low_s[...], m_high)
    for side in range(2):
        lanes = slice(side * LANES, side * LANES + LANES)
        parts = [values[g * share : (g + 1) * share, lanes] for g in range(GROUPS)]
        for n, block in enumerate(group_transpose(parts)):
            out_ref[side * GROUPS + n] = block


def arrive_kernel(got_ref, slot_ref, z_ref, solved_ref, top_ref, bottom_ref, west_ref, east_ref, r_s, g_s, sems):
    share = got_ref.shape[1]
    copies = [
        pltpu.make_async_copy(
            got_ref.at[pl.ds(tile * GROUPS, GROUPS)],
            g_s.at[pl.ds(tile * GROUPS, GROUPS)],
            sems.at[tile],
        )
        for tile in range(PEERS // GROUPS)
    ]
    for copy in copies:
        copy.start()
    for tile in range(PEERS // GROUPS):
        lanes = slice(tile * LANES, tile * LANES + LANES)
        copies[tile].wait()
        parts = [g_s[tile * GROUPS + n] for n in range(GROUPS)]
        for g, block in enumerate(group_transpose(parts)):
            rows = slice(g * share, (g + 1) * share)
            for piece in range(2):
                short = block.astype(BF16)
                r_s[piece, rows, lanes] = short
                block = block - short.astype(F32)
    slots = PEERS * CAP
    pick = (iota((slots, CELLS), 0) == slot_ref[...]).astype(BF16)
    solved = z_ref[...]
    solved = solved + (dot_nn(r_s[1], pick) + dot_nn(r_s[0], pick))
    solved_ref[...] = solved
    top_ref[...] = solved[:, 0:LON]
    bottom_ref[...] = solved[:, CELLS - LON :]
    row = iota((8, CELLS), 0)
    spot = iota((8, CELLS), 1)
    edge = (spot == (row % ROWS) * LON + (row // ROWS) * (LON - 1)).astype(F32)
    edges = dot_nt(edge, solved, HI)
    west_ref[...] = edges[0:ROWS]
    east_ref[...] = edges[ROWS:]


def stencil_kernel(
    solved_ref, north_ref, south_ref, west_ref, east_ref, stencil_ref, *rest, start, count
):
    out_ref, block_s, sems = rest[-3:]
    sides = jnp.transpose(jnp.concatenate([west_ref[...], east_ref[...]], axis=0))
    copies = []
    for part, low in enumerate(range(0, count, CHUNK)):
        size = min(CHUNK, count - low)
        used = slice(low, low + size)
        lane = iota((size, LON), 1)
        rows = [solved_ref[used, r * LON : (r + 1) * LON] for r in range(ROWS)]
        for r in range(ROWS):
            here = rows[r]
            north = north_ref[used, :] if r == 0 else rows[r - 1]
            south = south_ref[used, :] if r == ROWS - 1 else rows[r + 1]
            west = jnp.where(lane == 0, sides[used, r : r + 1], pltpu.roll(here, 1, 1))
            east = jnp.where(
                lane == LON - 1,
                sides[used, ROWS + r : ROWS + r + 1],
                pltpu.roll(here, LON - 1, 1),
            )
            result = here
            for n, side in enumerate((north, south, west, east)):
                coef = stencil_ref[n * ROWS + r : n * ROWS + r + 1, :]
                result = result + coef * (side - here)
            block_s[pl.ds(low * ROWS + r, size, stride=ROWS), :] = result
        copy = pltpu.make_async_copy(
            block_s.at[pl.ds(low * ROWS, size * ROWS), :],
            out_ref.at[pl.ds((start + low) * ROWS, size * ROWS), :],
            sems.at[part],
        )
        copy.start()
        copies.append(copy)
    for copy in copies:
        copy.wait()


def shape_of(*dims, dtype=F32):
    return jax.ShapeDtypeStruct(dims, dtype)


def shift(cells, axis, step):
    count = lax.axis_size(axis)
    pairs = [(i, i + step) for i in range(count) if 0 <= i + step < count]
    return lax.ppermute(cells, axis, pairs)


def on_device(
    fields_in, drag_rate, loss_rate, diffusivity, owner_col, anchor_cell, offsets, stencil
):
    flat_in = fields_in.reshape(FLAT * ROWS, LON)
    request, slot_index = pl.pallas_call(
        request_kernel,
        out_shape=(shape_of(PEERS, LANES), shape_of(1, CELLS, dtype=jnp.int32)),
        name="request",
    )(owner_col.reshape(1, CELLS), anchor_cell.reshape(1, CELLS), offsets)
    got = lax.all_to_all(request, "col", split_axis=0, concat_axis=0, tiled=True)
    rates, inverse = pl.pallas_call(
        inverse_kernel,
        out_shape=(shape_of(LEV_PAD, 8), shape_of(FIELDS, LEV_ROWS, LEV_PAD)),
        scratch_shapes=[
            pltpu.VMEM((8, LEV_PAD), F32),
            pltpu.VMEM((8, LEV_PAD), F32),
            pltpu.VMEM((LEV_PAD * 8, LANES), F32),
            pltpu.VMEM((LEV_PAD * 8, LANES), F32),
        ],
        name="inverse",
    )(drag_rate.reshape(1, LEV), loss_rate, diffusivity)

    def solve(moved):
        return pl.pallas_call(
            partial(solve_kernel, moved=moved),
            out_shape=tuple(shape_of(count, CELLS) for count in COUNTS),
            scratch_shapes=[pltpu.VMEM((FIELDS, LEV_PAD, CELLS), F32)],
            name="solve_moved" if moved else "solve_half",
        )(flat_in, rates, inverse)

    sources = solve(True)
    returned = []
    for share, source in zip(SHARES, sources):
        values = pl.pallas_call(
            owner_kernel,
            grid=(PEERS // GROUPS // 2,),
            in_specs=[
                pl.BlockSpec((2 * GROUPS, LANES), lambda i: (i, 0)),
                pl.BlockSpec((GROUPS * share, CELLS), lambda i: (0, 0)),
            ],
            out_specs=pl.BlockSpec((2 * GROUPS, share, LANES), lambda i: (i, 0, 0)),
            out_shape=shape_of(PEERS, share, LANES),
            scratch_shapes=[pltpu.VMEM((GROUPS * share, CELLS), BF16)] * 2,
            name="owner",
        )(got, source)
        returned.append(
            lax.all_to_all(values, "col", split_axis=0, concat_axis=0, tiled=True)
        )
    locals_ = solve(False)
    coefs = stencil.reshape(4 * ROWS, LON)
    out = None
    for start, count, back, local in zip(STARTS, COUNTS, returned, locals_):
        solved, top, bottom, west, east = pl.pallas_call(
            arrive_kernel,
            in_specs=[pl.BlockSpec(memory_space=pl.ANY)]
            + [pl.BlockSpec(memory_space=pltpu.VMEM)] * 2,
            out_shape=(
                shape_of(count, CELLS),
                shape_of(count, LON),
                shape_of(count, LON),
                shape_of(ROWS, count),
                shape_of(ROWS, count),
            ),
            scratch_shapes=[
                pltpu.VMEM((2, count, PEERS * CAP), BF16),
                pltpu.VMEM((PEERS, share, LANES), F32),
                pltpu.SemaphoreType.DMA((PEERS // GROUPS,)),
            ],
            name="arrive",
        )(back, slot_index, local)
        from_north = shift(bottom, "band", 1)
        from_south = shift(top, "band", -1)
        from_west = shift(east, "col", 1)
        from_east = shift(west, "col", -1)
        used = min(count, FLAT - start)
        whole = [] if out is None else [out]
        out = pl.pallas_call(
            partial(stencil_kernel, start=start, count=used),
            out_shape=shape_of(FLAT * ROWS, LON),
            in_specs=[pl.BlockSpec(memory_space=pltpu.VMEM)] * 6
            + [pl.BlockSpec(memory_space=pl.ANY)] * len(whole),
            out_specs=pl.BlockSpec(memory_space=pl.ANY),
            scratch_shapes=[pltpu.VMEM((used * ROWS, LON), F32), pltpu.SemaphoreType.DMA((GROUPS,))],
            input_output_aliases={6: 0} if whole else {},
            name="stencil",
        )(solved, from_north, from_south, from_west, from_east, coefs, *whole)
    return out.reshape(fields_in.shape)


def solution(mesh):
    in_specs = (
        P(None, None, "band", "col"),
        P(),
        P(),
        P(),
        P("band", "col", None),
        P("band", "col"),
        P(None, "band", "col"),
        P(None, "band", "col"),
    )
    out_specs = P(None, None, "band", "col")
    return jax.shard_map(
        on_device, mesh=mesh, in_specs=in_specs, out_specs=out_specs, check_vma=False
    )
```

time: 158 us -> 151 us (0.956)
  blocking collectives: 88 us -> 0 us
  waiting for transfers between devices: 5.99 us -> 78.6 us
  starting transfers between devices: 23.2 us -> 32.6 us
  Pallas kernels: 37.9 us -> 35.8 us
    all_to_all x1 -> x0, blocking collectives: 88 us -> none  [on_device(): lax.all_to_all(values, 'col', split_axis=0, concat_axis=0, tiled=True)]
    all_to_all x0 -> x1, waiting for transfers between devices: none -> 72.6 us  [on_device(): lax.all_to_all(values, 'col', split_axis=0, concat_axis=0, tiled=True)]
    all_to_all x0 -> x1, starting transfers between devices: none -> 9.76 us  [on_device(): lax.all_to_all(values, 'col', split_axis=0, concat_axis=0, tiled=True)]
    pallas_call x4 -> x6, Pallas kernels: 35.4 us -> 33.4 us  [the longest x1 8.61 us: on_device(): pl.pallas_call(arrive_kernel, in_specs=[pl.BlockSpec(memory_space=pl.ANY)...]
    unnamed x11 -> x12, local copies, waits for them, and re-layouts: 2.78 us -> 3.19 us
  transfers between devices with their start and end apart: 5 -> 6, of which waited for: 1 -> 2; matrix products, arithmetic and copies ran while one was open for 0% -> 0% of each run, Pallas kernels for 8% -> 8%
where the time goes in v1:
time: 151 us; the launch traced here: 150 us
  waiting for transfers between devices  78.6 us (52%)
  Pallas kernels  35.8 us (24%)
  starting transfers between devices  32.6 us (22%)
  local copies, waits for them, and re-layouts  3.19 us (2%)
    all_to_all x1, waiting for transfers between devices, on_device(): lax.all_to_all(values, 'col', split_axis=0, concat_axis=0, tiled=True)  72.6 us
    all_to_all x1, starting transfers between devices, on_device(): lax.all_to_all(request, 'col', split_axis=0, concat_axis=0, tiled=True)  11.5 us
    ppermute x4, starting transfers between devices, shift(): return lax.ppermute(cells, axis, pairs)  11.4 us
    all_to_all x1, starting transfers between devices, on_device(): lax.all_to_all(values, 'col', split_axis=0, concat_axis=0, tiled=True)  9.76 us
    pallas_call x1, Pallas kernels, on_device(): pl.pallas_call(arrive_kernel, in_specs=[pl.BlockSpec(memory_space=pl.ANY)...  8.61 us
    pallas_call x2, Pallas kernels, solve(): pl.pallas_call(partial(solve_kernel, moved=moved), out_shape=tuple((shape...  8.1 us
    pallas_call x1, Pallas kernels, on_device(): pl.pallas_call(owner_kernel, grid=(PEERS // GROUPS // 2,), in_specs=[pl.B...  7.53 us
    ppermute x4, waiting for transfers between devices, shift(): return lax.ppermute(cells, axis, pairs)  5.99 us
  transfers between devices with their start and end apart: 6, of which 2 were waited for; matrix products, arithmetic and copies ran while one was open for 0% of the time, Pallas kernels for 8%

profile of v1, /device:TPU:26, one launch (start us, length us, event | category | flops | bytes accessed | tf_op | source)
XLA Modules:
  0.0 150.3 jit_solution(17952010580314709242)
XLA Ops:
  0.0 2.4 %request.1 = (f32[32,128]{1,0:T(8,128)}, s32[1,512]{1,0:T(1,128)}) custom-call(s32[1,512]{1,0:T(1,128)} %bitcast.14, s32[1,512]{1,0:T(1,128)} %anchor_ref.1, f32[2,1,512]{2,1,0:T(1,128)} %offsets_ref.1), custom_call_target="tpu_custom_call" | custom-call | tf_op jit(solution)/shard_map/request/pallas_call | solution.py:313
  2.4 11.5 %all-to-all-start = ((f32[32,1,128]{2,1,0:T(1,128)}), f32[32,1,128]{2,1,0:T(1,128)S(1)}, u32[]{:S(2)}, u32[]{:S(2)}) async-start(f32[32,1,128]{2,1,0:T(1,128)} %bitcast.12), calls=%async_computation | async-start | bytes 32768 | tf_op jit(solution)/shard_map/all_to_all | solution.py:318
  13.9 4.3 %inverse.1 = (f32[256,8]{1,0:T(8,128)}, f32[6,144,256]{2,1,0:T(8,128)}) custom-call(f32[1,137]{1,0:T(1,128)} %bitcast.15, f32[4,137]{1,0:T(4,128)} %loss_ref.1, f32[6,136]{1,0:T(8,128)} %diff_ref.1), custom_call_target="tpu_custom_call" | custom-call | tf_op jit(solution)/shard_map/inverse/pallas_call | solution.py:319
  18.2 4.0 %solve_moved.1.y_ref = f32[832,512]{1,0:T(8,128)} custom-call(f32[3288,128]{1,0:T(8,128)} %bitcast.9, f32[256,8]{1,0:T(8,128)} %get-tuple-element.15.rate_ref, f32[6,144,256]{2,1,0:T(8,128)} %get-tuple-element.16.inverse_ref), custom_call_target="tpu_custom_call" | custom-call | tf_op jit(solution)/shard_map/solve_moved/pallas_call | solution.py:332
  22.2 0.0 all-to-all-done
  22.2 0.6 copy-done.3
  22.8 7.5 %owner.1 = f32[32,208,128]{2,1,0:T(8,128)} custom-call(f32[32,128]{1,0:T(8,128)} %bitcast.11, f32[832,512]{1,0:T(8,128)} %solve_moved.1.y_ref), custom_call_target="tpu_custom_call" | custom-call | tf_op jit(solution)/shard_map/owner/pallas_call | solution.py:342
  30.3 9.8 %all-to-all-start.1 = ((f32[32,208,128]{2,1,0:T(8,128)}), f32[32,208,128]{2,1,0:T(8,128)S(1)}, u32[]{:S(2)}, u32[]{:S(2)}) async-start(f32[32,208,128]{2,1,0:T(8,128)} %owner.1), calls=%async_computation.1 | async-start | bytes 6815744 | tf_op jit(solution)/shard_map/all_to_all | solution.py:355
  40.1 4.1 %solve_half.1.z_ref = f32[832,512]{1,0:T(8,128)} custom-call(f32[3288,128]{1,0:T(8,128)} %bitcast.10, f32[256,8]{1,0:T(8,128)} %get-tuple-element.15.rate_ref, f32[6,144,256]{2,1,0:T(8,128)} %get-tuple-element.16.inverse_ref), custom_call_target="tpu_custom_call" | custom-call | tf_op jit(solution)/shard_map/solve_half/pallas_call | solution.py:332
  44.2 72.6 %all-to-all-done.1.got_ref = f32[32,208,128]{2,1,0:T(8,128)S(1)} async-done(((f32[32,208,128]{2,1,0:T(8,128)}), f32[32,208,128]{2,1,0:T(8,128)S(1)}, u32[]{:S(2)}, u32[]{:S(2)}) %all-to-all-start.1) | async-done | bytes 3407904 | tf_op jit(solution)/shard_map/all_to_all | solution.py:355
  116.8 1.7 %copy-done = f32[32,208,128]{2,1,0:T(8,128)} copy-done((f32[32,208,128]{2,1,0:T(8,128)}, f32[32,208,128]{2,1,0:T(8,128)S(1)}, u32[]{:S(2)}) %copy-start) | copy-done | bytes 3407896
  118.5 8.6 %arrive.1 = (f32[832,512]{1,0:T(8,128)}, f32[832,128]{1,0:T(8,128)}, f32[832,128]{1,0:T(8,128)}, f32[4,832]{1,0:T(4,128)}, f32[4,832]{1,0:T(4,128)}) custom-call(f32[32,208,128]{2,1,0:T(8,128)} %copy-done, s32[1,512]{1,0:T(1,128)} %get-tuple-element.17.slot_ref, f32[832,512]{1,0:T(8,128)} %solve_half.1.z_ref), custom_call_target="tpu_custom_call" | custom-call | tf_op jit(solution)/shard_map/arrive/pallas_call | solution.py:361
  127.1 1.9 %collective-permute-start = (f32[832,128]{1,0:T(8,128)}, f32[832,128]{1,0:T(8,128)S(1)}, u32[]{:S(2)}, u32[]{:S(2)}) collective-permute-start(f32[832,128]{1,0:T(8,128)} %get-tuple-element.19), channel_id=1, source_target_pairs={{0,32},{32,64},{64,96},{96,128},{128,160},{160,192},{192,224},{1,3... | collective-permute-start | bytes 1277960 | tf_op jit(solution)/shard_map/ppermute | solution.py:306
  129.0 3.6 %collective-permute-start.1 = (f32[832,128]{1,0:T(8,128)}, f32[832,128]{1,0:T(8,128)S(1)}, u32[]{:S(2)}, u32[]{:S(2)}) collective-permute-start(f32[832,128]{1,0:T(8,128)} %get-tuple-element.20), channel_id=1, source_target_pairs={{32,0},{64,32},{96,64},{128,96},{160,128},{192,160},{224,192},{33,... | collective-permute-start | bytes 1277960 | tf_op jit(solution)/shard_map/ppermute | solution.py:306
  132.7 3.9 %collective-permute-start.2 = (f32[4,832]{1,0:T(4,128)}, f32[4,832]{1,0:T(4,128)S(1)}, u32[]{:S(2)}, u32[]{:S(2)}) collective-permute-start(f32[4,832]{1,0:T(4,128)} %get-tuple-element.21), channel_id=1, source_target_pairs={{0,1},{1,2},{2,3},{3,4},{4,5},{5,6},{6,7},{7,8},{8,9},{9,10},{10,1... | collective-permute-start | bytes 39944 | tf_op jit(solution)/shard_map/ppermute | solution.py:306
  136.6 1.9 %collective-permute-start.3 = (f32[4,832]{1,0:T(4,128)}, f32[4,832]{1,0:T(4,128)S(1)}, u32[]{:S(2)}, u32[]{:S(2)}) collective-permute-start(f32[4,832]{1,0:T(4,128)} %get-tuple-element.22), channel_id=1, source_target_pairs={{1,0},{2,1},{3,2},{4,3},{5,4},{6,5},{7,6},{8,7},{9,8},{10,9},{11,1... | collective-permute-start | bytes 39944 | tf_op jit(solution)/shard_map/ppermute | solution.py:306
  138.5 0.0 collective-permute-done.2.west_ref
  138.6 6.0 %collective-permute-done.3.east_ref = f32[4,832]{1,0:T(4,128)S(1)} collective-permute-done((f32[4,832]{1,0:T(4,128)}, f32[4,832]{1,0:T(4,128)S(1)}, u32[]{:S(2)}, u32[]{:S(2)}) %collective-permute-start.3) | collective-permute-done | bytes 13344 | tf_op jit(solution)/shard_map/ppermute | solution.py:306
  144.5 0.0 collective-permute-done.north_ref
  144.5 0.0 collective-permute-done.1.south_ref
  144.6 0.6 copy-done.5
  145.1 0.2 copy-done.1
  145.3 0.1 copy-done.2
  145.4 4.9 %stencil.1 = f32[3288,128]{1,0:T(8,128)} custom-call(f32[832,512]{1,0:T(8,128)} %get-tuple-element.18.solved_ref, f32[832,128]{1,0:T(8,128)} %copy-done.1, f32[832,128]{1,0:T(8,128)} %copy-done.2, f32[4,832]{1,0:T(4,128)} %copy-done.4, f32[4,832]{1,0:T(4,128)} %copy-done.5, f32[16,128]{1,0:T(8,128)} %bitcast.13), custom_call_target="tpu_custom_call" | custom-call | tf_op jit(solution)/shard_map/stencil/pallas_call | solution.py:385
  (7 shorter events, 0.0 us)
Async XLA Ops:
  2.4 19.8 %all-to-all-start = ((f32[32,1,128]{2,1,0:T(1,128)}), f32[32,1,128]{2,1,0:T(1,128)S(1)}, u32[]{:S(2)}, u32[]{:S(2)}) async-start(f32[32,1,128]{2,1,0:T(1,128)} %bitcast.12), calls=%async_computation | async-start | bytes 32768 | tf_op jit(solution)/shard_map/all_to_all | solution.py:318
  22.2 0.6 copy-start.3
  30.3 86.4 %all-to-all-start.1 = ((f32[32,208,128]{2,1,0:T(8,128)}), f32[32,208,128]{2,1,0:T(8,128)S(1)}, u32[]{:S(2)}, u32[]{:S(2)}) async-start(f32[32,208,128]{2,1,0:T(8,128)} %owner.1), calls=%async_computation.1 | async-start | bytes 6815744 | tf_op jit(solution)/shard_map/all_to_all | solution.py:355
  116.8 1.7 %copy-start = (f32[32,208,128]{2,1,0:T(8,128)}, f32[32,208,128]{2,1,0:T(8,128)S(1)}, u32[]{:S(2)}) copy-start(f32[32,208,128]{2,1,0:T(8,128)S(1)} %all-to-all-done.1.got_ref) | copy-start | bytes 10223620
  127.1 17.4 %collective-permute-start = (f32[832,128]{1,0:T(8,128)}, f32[832,128]{1,0:T(8,128)S(1)}, u32[]{:S(2)}, u32[]{:S(2)}) collective-permute-start(f32[832,128]{1,0:T(8,128)} %get-tuple-element.19), channel_id=1, source_target_pairs={{0,32},{32,64},{64,96},{96,128},{128,160},{160,192},{192,224},{1,3... | collective-permute-start | bytes 1277960 | tf_op jit(solution)/shard_map/ppermute | solution.py:306
  129.0 15.5 %collective-permute-start.1 = (f32[832,128]{1,0:T(8,128)}, f32[832,128]{1,0:T(8,128)S(1)}, u32[]{:S(2)}, u32[]{:S(2)}) collective-permute-start(f32[832,128]{1,0:T(8,128)} %get-tuple-element.20), channel_id=1, source_target_pairs={{32,0},{64,32},{96,64},{128,96},{160,128},{192,160},{224,192},{33,... | collective-permute-start | bytes 1277960 | tf_op jit(solution)/shard_map/ppermute | solution.py:306
  132.7 5.9 %collective-permute-start.2 = (f32[4,832]{1,0:T(4,128)}, f32[4,832]{1,0:T(4,128)S(1)}, u32[]{:S(2)}, u32[]{:S(2)}) collective-permute-start(f32[4,832]{1,0:T(4,128)} %get-tuple-element.21), channel_id=1, source_target_pairs={{0,1},{1,2},{2,3},{3,4},{4,5},{5,6},{6,7},{7,8},{8,9},{9,10},{10,1... | collective-permute-start | bytes 39944 | tf_op jit(solution)/shard_map/ppermute | solution.py:306
  136.6 7.9 %collective-permute-start.3 = (f32[4,832]{1,0:T(4,128)}, f32[4,832]{1,0:T(4,128)S(1)}, u32[]{:S(2)}, u32[]{:S(2)}) collective-permute-start(f32[4,832]{1,0:T(4,128)} %get-tuple-element.22), channel_id=1, source_target_pairs={{1,0},{2,1},{3,2},{4,3},{5,4},{6,5},{7,6},{8,7},{9,8},{10,9},{11,1... | collective-permute-start | bytes 39944 | tf_op jit(solution)/shard_map/ppermute | solution.py:306
  138.5 6.0 %copy-start.4 = (f32[4,832]{1,0:T(4,128)}, f32[4,832]{1,0:T(4,128)S(1)}, u32[]{:S(2)}) copy-start(f32[4,832]{1,0:T(4,128)S(1)} %collective-permute-done.2.west_ref) | copy-start | bytes 39940
  144.5 0.6 copy-start.5
  144.5 0.8 copy-start.1
  144.6 0.9 copy-start.2

commit v2 on v1

--- a/solution.py
+++ b/solution.py
@@ -333,6 +333,7 @@
             partial(solve_kernel, moved=moved),
             out_shape=tuple(shape_of(count, CELLS) for count in COUNTS),
             scratch_shapes=[pltpu.VMEM((FIELDS, LEV_PAD, CELLS), F32)],
+            compiler_params=None if moved else pltpu.CompilerParams(vmem_limit_bytes=65_000_000),
             name="solve_moved" if moved else "solve_half",
         )(flat_in, rates, inverse)
 

time: 151 us -> 149 us (0.987)
  local copies, waits for them, and re-layouts: 3.19 us -> 1.48 us
    unnamed x12 -> x10, local copies, waits for them, and re-layouts: 3.19 us -> 1.48 us
where the time goes in v2:
time: 149 us
  waiting for transfers between devices  78.4 us (53%)
  Pallas kernels  35.8 us (24%)
  starting transfers between devices  32.9 us (22%)
    all_to_all x1, waiting for transfers between devices, on_device(): lax.all_to_all(values, 'col', split_axis=0, concat_axis=0, tiled=True)  72.6 us
    ppermute x4, starting transfers between devices, shift(): return lax.ppermute(cells, axis, pairs)  11.6 us
    all_to_all x1, starting transfers between devices, on_device(): lax.all_to_all(request, 'col', split_axis=0, concat_axis=0, tiled=True)  11.5 us
    all_to_all x1, starting transfers between devices, on_device(): lax.all_to_all(values, 'col', split_axis=0, concat_axis=0, tiled=True)  9.83 us
    pallas_call x1, Pallas kernels, on_device(): pl.pallas_call(arrive_kernel, in_specs=[pl.BlockSpec(memory_space=pl.ANY)...  8.61 us
    pallas_call x2, Pallas kernels, solve(): pl.pallas_call(partial(solve_kernel, moved=moved), out_shape=tuple((shape...  8.14 us
    pallas_call x1, Pallas kernels, on_device(): pl.pallas_call(owner_kernel, grid=(PEERS // GROUPS // 2,), in_specs=[pl.B...  7.53 us
    ppermute x4, waiting for transfers between devices, shift(): return lax.ppermute(cells, axis, pairs)  5.75 us
  transfers between devices with their start and end apart: 6, of which 2 were waited for; matrix products, arithmetic and copies ran while one was open for 0% of the time, Pallas kernels for 8%

profile of v2, /device:TPU:26, one launch (start us, length us, event | category | flops | bytes accessed | tf_op | source)
XLA Modules:
  0.0 148.7 jit_solution(9475841329072535126)
XLA Ops:
  0.0 2.4 %request.1 = (f32[32,128]{1,0:T(8,128)}, s32[1,512]{1,0:T(1,128)}) custom-call(s32[1,512]{1,0:T(1,128)} %bitcast.14, s32[1,512]{1,0:T(1,128)} %anchor_ref.1, f32[2,1,512]{2,1,0:T(1,128)} %offsets_ref.1), custom_call_target="tpu_custom_call" | custom-call | tf_op jit(solution)/shard_map/request/pallas_call | solution.py:313
  2.4 11.5 %all-to-all-start = ((f32[32,1,128]{2,1,0:T(1,128)}), f32[32,1,128]{2,1,0:T(1,128)S(1)}, u32[]{:S(2)}, u32[]{:S(2)}) async-start(f32[32,1,128]{2,1,0:T(1,128)} %bitcast.12), calls=%async_computation | async-start | bytes 32768 | tf_op jit(solution)/shard_map/all_to_all | solution.py:318
  13.9 4.3 %inverse.1 = (f32[256,8]{1,0:T(8,128)}, f32[6,144,256]{2,1,0:T(8,128)}) custom-call(f32[1,137]{1,0:T(1,128)} %bitcast.15, f32[4,137]{1,0:T(4,128)} %loss_ref.1, f32[6,136]{1,0:T(8,128)} %diff_ref.1), custom_call_target="tpu_custom_call" | custom-call | tf_op jit(solution)/shard_map/inverse/pallas_call | solution.py:319
  18.2 4.0 %solve_moved.1.y_ref = f32[832,512]{1,0:T(8,128)} custom-call(f32[3288,128]{1,0:T(8,128)} %bitcast.9, f32[256,8]{1,0:T(8,128)} %get-tuple-element.15.rate_ref, f32[6,144,256]{2,1,0:T(8,128)} %get-tuple-element.16.inverse_ref), custom_call_target="tpu_custom_call" | custom-call | tf_op jit(solution)/shard_map/solve_moved/pallas_call | solution.py:332
  22.2 0.0 all-to-all-done
  22.2 0.6 copy-done.2
  22.8 7.5 %owner.1 = f32[32,208,128]{2,1,0:T(8,128)} custom-call(f32[32,128]{1,0:T(8,128)} %bitcast.11, f32[832,512]{1,0:T(8,128)} %solve_moved.1.y_ref), custom_call_target="tpu_custom_call" | custom-call | tf_op jit(solution)/shard_map/owner/pallas_call | solution.py:343
  30.3 9.8 %all-to-all-start.1 = ((f32[32,208,128]{2,1,0:T(8,128)}), f32[32,208,128]{2,1,0:T(8,128)}, u32[]{:S(2)}, u32[]{:S(2)}) async-start(f32[32,208,128]{2,1,0:T(8,128)} %owner.1), calls=%async_computation.1 | async-start | bytes 6815744 | tf_op jit(solution)/shard_map/all_to_all | solution.py:356
  40.2 4.1 %solve_half.1.z_ref = f32[832,512]{1,0:T(8,128)} custom-call(f32[3288,128]{1,0:T(8,128)} %bitcast.10, f32[256,8]{1,0:T(8,128)} %get-tuple-element.15.rate_ref, f32[6,144,256]{2,1,0:T(8,128)} %get-tuple-element.16.inverse_ref), custom_call_target="tpu_custom_call" | custom-call | tf_op jit(solution)/shard_map/solve_half/pallas_call | solution.py:332
  44.3 72.6 %all-to-all-done.1.got_ref = f32[32,208,128]{2,1,0:T(8,128)} async-done(((f32[32,208,128]{2,1,0:T(8,128)}), f32[32,208,128]{2,1,0:T(8,128)}, u32[]{:S(2)}, u32[]{:S(2)}) %all-to-all-start.1) | async-done | bytes 3407904 | tf_op jit(solution)/shard_map/all_to_all | solution.py:356
  116.9 8.6 %arrive.1 = (f32[832,512]{1,0:T(8,128)}, f32[832,128]{1,0:T(8,128)}, f32[832,128]{1,0:T(8,128)}, f32[4,832]{1,0:T(4,128)}, f32[4,832]{1,0:T(4,128)}) custom-call(f32[32,208,128]{2,1,0:T(8,128)} %all-to-all-done.1.got_ref, s32[1,512]{1,0:T(1,128)} %get-tuple-element.17.slot_ref, f32[832,512]{1,0:T(8,128)} %solve_half.1.z_ref), custom_call_target="tpu_custom_call" | custom-call | tf_op jit(solution)/shard_map/arrive/pallas_call | solution.py:362
  125.5 1.9 %collective-permute-start = (f32[832,128]{1,0:T(8,128)}, f32[832,128]{1,0:T(8,128)S(1)}, u32[]{:S(2)}, u32[]{:S(2)}) collective-permute-start(f32[832,128]{1,0:T(8,128)} %get-tuple-element.19), channel_id=1, source_target_pairs={{0,32},{32,64},{64,96},{96,128},{128,160},{160,192},{192,224},{1,3... | collective-permute-start | bytes 1277960 | tf_op jit(solution)/shard_map/ppermute | solution.py:306
  127.4 3.6 %collective-permute-start.1 = (f32[832,128]{1,0:T(8,128)}, f32[832,128]{1,0:T(8,128)S(1)}, u32[]{:S(2)}, u32[]{:S(2)}) collective-permute-start(f32[832,128]{1,0:T(8,128)} %get-tuple-element.20), channel_id=1, source_target_pairs={{32,0},{64,32},{96,64},{128,96},{160,128},{192,160},{224,192},{33,... | collective-permute-start | bytes 1277960 | tf_op jit(solution)/shard_map/ppermute | solution.py:306
  131.1 3.9 %collective-permute-start.2 = (f32[4,832]{1,0:T(4,128)}, f32[4,832]{1,0:T(4,128)S(1)}, u32[]{:S(2)}, u32[]{:S(2)}) collective-permute-start(f32[4,832]{1,0:T(4,128)} %get-tuple-element.21), channel_id=1, source_target_pairs={{0,1},{1,2},{2,3},{3,4},{4,5},{5,6},{6,7},{7,8},{8,9},{9,10},{10,1... | collective-permute-start | bytes 39944 | tf_op jit(solution)/shard_map/ppermute | solution.py:306
  135.0 2.2 %collective-permute-start.3 = (f32[4,832]{1,0:T(4,128)}, f32[4,832]{1,0:T(4,128)S(1)}, u32[]{:S(2)}, u32[]{:S(2)}) collective-permute-start(f32[4,832]{1,0:T(4,128)} %get-tuple-element.22), channel_id=1, source_target_pairs={{1,0},{2,1},{3,2},{4,3},{5,4},{6,5},{7,6},{8,7},{9,8},{10,9},{11,1... | collective-permute-start | bytes 39944 | tf_op jit(solution)/shard_map/ppermute | solution.py:306
  137.2 0.0 collective-permute-done.2.west_ref
  137.2 0.0 copy-start.3
  137.2 5.7 %collective-permute-done.3.east_ref = f32[4,832]{1,0:T(4,128)S(1)} collective-permute-done((f32[4,832]{1,0:T(4,128)}, f32[4,832]{1,0:T(4,128)S(1)}, u32[]{:S(2)}, u32[]{:S(2)}) %collective-permute-start.3) | collective-permute-done | bytes 13344 | tf_op jit(solution)/shard_map/ppermute | solution.py:306
  143.0 0.0 collective-permute-done.north_ref
  143.0 0.0 collective-permute-done.1.south_ref
  143.0 0.6 copy-done.4
  143.5 0.2 copy-done
  143.7 0.1 copy-done.1
  143.9 4.9 %stencil.1 = f32[3288,128]{1,0:T(8,128)} custom-call(f32[832,512]{1,0:T(8,128)} %get-tuple-element.18.solved_ref, f32[832,128]{1,0:T(8,128)} %copy-done, f32[832,128]{1,0:T(8,128)} %copy-done.1, f32[4,832]{1,0:T(4,128)} %copy-done.3, f32[4,832]{1,0:T(4,128)} %copy-done.4, f32[16,128]{1,0:T(8,128)} %bitcast.13), custom_call_target="tpu_custom_call" | custom-call | tf_op jit(solution)/shard_map/stencil/pallas_call | solution.py:386
  (5 shorter events, 0.0 us)
Async XLA Ops:
  2.4 19.8 %all-to-all-start = ((f32[32,1,128]{2,1,0:T(1,128)}), f32[32,1,128]{2,1,0:T(1,128)S(1)}, u32[]{:S(2)}, u32[]{:S(2)}) async-start(f32[32,1,128]{2,1,0:T(1,128)} %bitcast.12), calls=%async_computation | async-start | bytes 32768 | tf_op jit(solution)/shard_map/all_to_all | solution.py:318
  22.2 0.6 copy-start.2
  30.3 86.6 %all-to-all-start.1 = ((f32[32,208,128]{2,1,0:T(8,128)}), f32[32,208,128]{2,1,0:T(8,128)}, u32[]{:S(2)}, u32[]{:S(2)}) async-start(f32[32,208,128]{2,1,0:T(8,128)} %owner.1), calls=%async_computation.1 | async-start | bytes 6815744 | tf_op jit(solution)/shard_map/all_to_all | solution.py:356
  125.5 17.4 %collective-permute-start = (f32[832,128]{1,0:T(8,128)}, f32[832,128]{1,0:T(8,128)S(1)}, u32[]{:S(2)}, u32[]{:S(2)}) collective-permute-start(f32[832,128]{1,0:T(8,128)} %get-tuple-element.19), channel_id=1, source_target_pairs={{0,32},{32,64},{64,96},{96,128},{128,160},{160,192},{192,224},{1,3... | collective-permute-start | bytes 1277960 | tf_op jit(solution)/shard_map/ppermute | solution.py:306
  127.4 15.5 %collective-permute-start.1 = (f32[832,128]{1,0:T(8,128)}, f32[832,128]{1,0:T(8,128)S(1)}, u32[]{:S(2)}, u32[]{:S(2)}) collective-permute-start(f32[832,128]{1,0:T(8,128)} %get-tuple-element.20), channel_id=1, source_target_pairs={{32,0},{64,32},{96,64},{128,96},{160,128},{192,160},{224,192},{33,... | collective-permute-start | bytes 1277960 | tf_op jit(solution)/shard_map/ppermute | solution.py:306
  131.1 6.1 %collective-permute-start.2 = (f32[4,832]{1,0:T(4,128)}, f32[4,832]{1,0:T(4,128)S(1)}, u32[]{:S(2)}, u32[]{:S(2)}) collective-permute-start(f32[4,832]{1,0:T(4,128)} %get-tuple-element.21), channel_id=1, source_target_pairs={{0,1},{1,2},{2,3},{3,4},{4,5},{5,6},{6,7},{7,8},{8,9},{9,10},{10,1... | collective-permute-start | bytes 39944 | tf_op jit(solution)/shard_map/ppermute | solution.py:306
  135.0 7.9 %collective-permute-start.3 = (f32[4,832]{1,0:T(4,128)}, f32[4,832]{1,0:T(4,128)S(1)}, u32[]{:S(2)}, u32[]{:S(2)}) collective-permute-start(f32[4,832]{1,0:T(4,128)} %get-tuple-element.22), channel_id=1, source_target_pairs={{1,0},{2,1},{3,2},{4,3},{5,4},{6,5},{7,6},{8,7},{9,8},{10,9},{11,1... | collective-permute-start | bytes 39944 | tf_op jit(solution)/shard_map/ppermute | solution.py:306
  137.2 5.8 %copy-start.3 = (f32[4,832]{1,0:T(4,128)}, f32[4,832]{1,0:T(4,128)S(1)}, u32[]{:S(2)}) copy-start(f32[4,832]{1,0:T(4,128)S(1)} %collective-permute-done.2.west_ref) | copy-start | bytes 39940
  142.9 0.6 copy-start.4
  143.0 0.8 copy-start
  143.0 0.9 copy-start.1

commit v3 on v1

--- a/solution.py
+++ b/solution.py
@@ -333,6 +333,9 @@
             partial(solve_kernel, moved=moved),
             out_shape=tuple(shape_of(count, CELLS) for count in COUNTS),
             scratch_shapes=[pltpu.VMEM((FIELDS, LEV_PAD, CELLS), F32)],
+            compiler_params=pltpu.CompilerParams(
+                vmem_limit_bytes=67_100_000 if moved else 65_000_000
+            ),
             name="solve_moved" if moved else "solve_half",
         )(flat_in, rates, inverse)
 

time: 151 us -> 149 us (0.987)
  local copies, waits for them, and re-layouts: 3.19 us -> 0.89 us
    unnamed x12 -> x8, local copies, waits for them, and re-layouts: 3.19 us -> 0.89 us
where the time goes in v3:
time: 149 us; the launch traced here: 148 us
  waiting for transfers between devices  78.6 us (53%)
  Pallas kernels  35.8 us (24%)
  starting transfers between devices  32.8 us (22%)
    all_to_all x1, waiting for transfers between devices, on_device(): lax.all_to_all(values, 'col', split_axis=0, concat_axis=0, tiled=True)  72.6 us
    all_to_all x1, starting transfers between devices, on_device(): lax.all_to_all(request, 'col', split_axis=0, concat_axis=0, tiled=True)  11.5 us
    ppermute x4, starting transfers between devices, shift(): return lax.ppermute(cells, axis, pairs)  11.4 us
    all_to_all x1, starting transfers between devices, on_device(): lax.all_to_all(values, 'col', split_axis=0, concat_axis=0, tiled=True)  9.83 us
    pallas_call x1, Pallas kernels, on_device(): pl.pallas_call(arrive_kernel, in_specs=[pl.BlockSpec(memory_space=pl.ANY)...  8.61 us
    pallas_call x2, Pallas kernels, solve(): pl.pallas_call(partial(solve_kernel, moved=moved), out_shape=tuple((shape...  8.13 us
    pallas_call x1, Pallas kernels, on_device(): pl.pallas_call(owner_kernel, grid=(PEERS // GROUPS // 2,), in_specs=[pl.B...  7.52 us
    ppermute x4, waiting for transfers between devices, shift(): return lax.ppermute(cells, axis, pairs)  5.99 us
  transfers between devices with their start and end apart: 6, of which 2 were waited for; matrix products, arithmetic and copies ran while one was open for 0% of the time, Pallas kernels for 8%

profile of v3, /device:TPU:26, one launch (start us, length us, event | category | flops | bytes accessed | tf_op | source)
XLA Modules:
  0.0 148.2 jit_solution(5625599985691480855)
XLA Ops:
  0.0 2.4 %request.1 = (f32[32,128]{1,0:T(8,128)}, s32[1,512]{1,0:T(1,128)}) custom-call(s32[1,512]{1,0:T(1,128)} %bitcast.13, s32[1,512]{1,0:T(1,128)} %anchor_ref.1, f32[2,1,512]{2,1,0:T(1,128)} %offsets_ref.1), custom_call_target="tpu_custom_call" | custom-call | tf_op jit(solution)/shard_map/request/pallas_call | solution.py:313
  2.4 11.5 %all-to-all-start = ((f32[32,1,128]{2,1,0:T(1,128)}), f32[32,1,128]{2,1,0:T(1,128)}, u32[]{:S(2)}, u32[]{:S(2)}) async-start(f32[32,1,128]{2,1,0:T(1,128)} %bitcast.11), calls=%async_computation | async-start | bytes 32768 | tf_op jit(solution)/shard_map/all_to_all | solution.py:318
  14.0 4.3 %inverse.1 = (f32[256,8]{1,0:T(8,128)}, f32[6,144,256]{2,1,0:T(8,128)}) custom-call(f32[1,137]{1,0:T(1,128)} %bitcast.14, f32[4,137]{1,0:T(4,128)} %loss_ref.1, f32[6,136]{1,0:T(8,128)} %diff_ref.1), custom_call_target="tpu_custom_call" | custom-call | tf_op jit(solution)/shard_map/inverse/pallas_call | solution.py:319
  18.2 4.0 %solve_moved.1.y_ref = f32[832,512]{1,0:T(8,128)} custom-call(f32[3288,128]{1,0:T(8,128)} %bitcast.9, f32[256,8]{1,0:T(8,128)} %get-tuple-element.15.rate_ref, f32[6,144,256]{2,1,0:T(8,128)} %get-tuple-element.16.inverse_ref), custom_call_target="tpu_custom_call" | custom-call | tf_op jit(solution)/shard_map/solve_moved/pallas_call | solution.py:332
  22.3 0.0 all-to-all-done
  22.3 7.5 %owner.1 = f32[32,208,128]{2,1,0:T(8,128)} custom-call(f32[32,128]{1,0:T(8,128)} %bitcast.3.got_ref, f32[832,512]{1,0:T(8,128)} %solve_moved.1.y_ref), custom_call_target="tpu_custom_call" | custom-call | tf_op jit(solution)/shard_map/owner/pallas_call | solution.py:345
  29.8 9.8 %all-to-all-start.1 = ((f32[32,208,128]{2,1,0:T(8,128)}), f32[32,208,128]{2,1,0:T(8,128)}, u32[]{:S(2)}, u32[]{:S(2)}) async-start(f32[32,208,128]{2,1,0:T(8,128)} %owner.1), calls=%async_computation.1 | async-start | bytes 6815744 | tf_op jit(solution)/shard_map/all_to_all | solution.py:358
  39.6 4.1 %solve_half.1.z_ref = f32[832,512]{1,0:T(8,128)} custom-call(f32[3288,128]{1,0:T(8,128)} %bitcast.10, f32[256,8]{1,0:T(8,128)} %get-tuple-element.15.rate_ref, f32[6,144,256]{2,1,0:T(8,128)} %get-tuple-element.16.inverse_ref), custom_call_target="tpu_custom_call" | custom-call | tf_op jit(solution)/shard_map/solve_half/pallas_call | solution.py:332
  43.7 72.6 %all-to-all-done.1.got_ref = f32[32,208,128]{2,1,0:T(8,128)} async-done(((f32[32,208,128]{2,1,0:T(8,128)}), f32[32,208,128]{2,1,0:T(8,128)}, u32[]{:S(2)}, u32[]{:S(2)}) %all-to-all-start.1) | async-done | bytes 3407904 | tf_op jit(solution)/shard_map/all_to_all | solution.py:358
  116.3 8.6 %arrive.1 = (f32[832,512]{1,0:T(8,128)}, f32[832,128]{1,0:T(8,128)}, f32[832,128]{1,0:T(8,128)}, f32[4,832]{1,0:T(4,128)}, f32[4,832]{1,0:T(4,128)}) custom-call(f32[32,208,128]{2,1,0:T(8,128)} %all-to-all-done.1.got_ref, s32[1,512]{1,0:T(1,128)} %get-tuple-element.17.slot_ref, f32[832,512]{1,0:T(8,128)} %solve_half.1.z_ref), custom_call_target="tpu_custom_call" | custom-call | tf_op jit(solution)/shard_map/arrive/pallas_call | solution.py:364
  125.0 1.9 %collective-permute-start = (f32[832,128]{1,0:T(8,128)}, f32[832,128]{1,0:T(8,128)S(1)}, u32[]{:S(2)}, u32[]{:S(2)}) collective-permute-start(f32[832,128]{1,0:T(8,128)} %get-tuple-element.19), channel_id=1, source_target_pairs={{0,32},{32,64},{64,96},{96,128},{128,160},{160,192},{192,224},{1,3... | collective-permute-start | bytes 1277960 | tf_op jit(solution)/shard_map/ppermute | solution.py:306
  126.9 3.6 %collective-permute-start.1 = (f32[832,128]{1,0:T(8,128)}, f32[832,128]{1,0:T(8,128)S(1)}, u32[]{:S(2)}, u32[]{:S(2)}) collective-permute-start(f32[832,128]{1,0:T(8,128)} %get-tuple-element.20), channel_id=1, source_target_pairs={{32,0},{64,32},{96,64},{128,96},{160,128},{192,160},{224,192},{33,... | collective-permute-start | bytes 1277960 | tf_op jit(solution)/shard_map/ppermute | solution.py:306
  130.5 3.9 %collective-permute-start.2 = (f32[4,832]{1,0:T(4,128)}, f32[4,832]{1,0:T(4,128)S(1)}, u32[]{:S(2)}, u32[]{:S(2)}) collective-permute-start(f32[4,832]{1,0:T(4,128)} %get-tuple-element.21), channel_id=1, source_target_pairs={{0,1},{1,2},{2,3},{3,4},{4,5},{5,6},{6,7},{7,8},{8,9},{9,10},{10,1... | collective-permute-start | bytes 39944 | tf_op jit(solution)/shard_map/ppermute | solution.py:306
  134.5 1.9 %collective-permute-start.3 = (f32[4,832]{1,0:T(4,128)}, f32[4,832]{1,0:T(4,128)S(1)}, u32[]{:S(2)}, u32[]{:S(2)}) collective-permute-start(f32[4,832]{1,0:T(4,128)} %get-tuple-element.22), channel_id=1, source_target_pairs={{1,0},{2,1},{3,2},{4,3},{5,4},{6,5},{7,6},{8,7},{9,8},{10,9},{11,1... | collective-permute-start | bytes 39944 | tf_op jit(solution)/shard_map/ppermute | solution.py:306
  136.4 0.0 collective-permute-done.2.west_ref
  136.4 0.0 copy-start.2
  136.4 6.0 %collective-permute-done.3.east_ref = f32[4,832]{1,0:T(4,128)S(1)} collective-permute-done((f32[4,832]{1,0:T(4,128)}, f32[4,832]{1,0:T(4,128)S(1)}, u32[]{:S(2)}, u32[]{:S(2)}) %collective-permute-start.3) | collective-permute-done | bytes 13344 | tf_op jit(solution)/shard_map/ppermute | solution.py:306
  142.4 0.0 collective-permute-done.north_ref
  142.4 0.0 collective-permute-done.1.south_ref
  142.4 0.0 copy-start.1
  142.4 0.6 copy-done.3
  143.0 0.2 copy-done
  143.2 0.1 copy-done.1
  143.3 4.9 %stencil.1 = f32[3288,128]{1,0:T(8,128)} custom-call(f32[832,512]{1,0:T(8,128)} %get-tuple-element.18.solved_ref, f32[832,128]{1,0:T(8,128)} %copy-done, f32[832,128]{1,0:T(8,128)} %copy-done.1, f32[4,832]{1,0:T(4,128)} %copy-done.2, f32[4,832]{1,0:T(4,128)} %copy-done.3, f32[16,128]{1,0:T(8,128)} %bitcast.12), custom_call_target="tpu_custom_call" | custom-call | tf_op jit(solution)/shard_map/stencil/pallas_call | solution.py:388
  (3 shorter events, 0.0 us)
Async XLA Ops:
  2.4 19.8 %all-to-all-start = ((f32[32,1,128]{2,1,0:T(1,128)}), f32[32,1,128]{2,1,0:T(1,128)}, u32[]{:S(2)}, u32[]{:S(2)}) async-start(f32[32,1,128]{2,1,0:T(1,128)} %bitcast.11), calls=%async_computation | async-start | bytes 32768 | tf_op jit(solution)/shard_map/all_to_all | solution.py:318
  29.8 86.6 %all-to-all-start.1 = ((f32[32,208,128]{2,1,0:T(8,128)}), f32[32,208,128]{2,1,0:T(8,128)}, u32[]{:S(2)}, u32[]{:S(2)}) async-start(f32[32,208,128]{2,1,0:T(8,128)} %owner.1), calls=%async_computation.1 | async-start | bytes 6815744 | tf_op jit(solution)/shard_map/all_to_all | solution.py:358
  125.0 17.5 %collective-permute-start = (f32[832,128]{1,0:T(8,128)}, f32[832,128]{1,0:T(8,128)S(1)}, u32[]{:S(2)}, u32[]{:S(2)}) collective-permute-start(f32[832,128]{1,0:T(8,128)} %get-tuple-element.19), channel_id=1, source_target_pairs={{0,32},{32,64},{64,96},{96,128},{128,160},{160,192},{192,224},{1,3... | collective-permute-start | bytes 1277960 | tf_op jit(solution)/shard_map/ppermute | solution.py:306
  126.9 15.5 %collective-permute-start.1 = (f32[832,128]{1,0:T(8,128)}, f32[832,128]{1,0:T(8,128)S(1)}, u32[]{:S(2)}, u32[]{:S(2)}) collective-permute-start(f32[832,128]{1,0:T(8,128)} %get-tuple-element.20), channel_id=1, source_target_pairs={{32,0},{64,32},{96,64},{128,96},{160,128},{192,160},{224,192},{33,... | collective-permute-start | bytes 1277960 | tf_op jit(solution)/shard_map/ppermute | solution.py:306
  130.5 5.9 %collective-permute-start.2 = (f32[4,832]{1,0:T(4,128)}, f32[4,832]{1,0:T(4,128)S(1)}, u32[]{:S(2)}, u32[]{:S(2)}) collective-permute-start(f32[4,832]{1,0:T(4,128)} %get-tuple-element.21), channel_id=1, source_target_pairs={{0,1},{1,2},{2,3},{3,4},{4,5},{5,6},{6,7},{7,8},{8,9},{9,10},{10,1... | collective-permute-start | bytes 39944 | tf_op jit(solution)/shard_map/ppermute | solution.py:306
  134.5 7.9 %collective-permute-start.3 = (f32[4,832]{1,0:T(4,128)}, f32[4,832]{1,0:T(4,128)S(1)}, u32[]{:S(2)}, u32[]{:S(2)}) collective-permute-start(f32[4,832]{1,0:T(4,128)} %get-tuple-element.22), channel_id=1, source_target_pairs={{1,0},{2,1},{3,2},{4,3},{5,4},{6,5},{7,6},{8,7},{9,8},{10,9},{11,1... | collective-permute-start | bytes 39944 | tf_op jit(solution)/shard_map/ppermute | solution.py:306
  136.4 6.0 %copy-start.2 = (f32[4,832]{1,0:T(4,128)}, f32[4,832]{1,0:T(4,128)S(1)}, u32[]{:S(2)}) copy-start(f32[4,832]{1,0:T(4,128)S(1)} %collective-permute-done.2.west_ref) | copy-start | bytes 39940
  142.4 0.6 copy-start.3
  142.4 0.8 copy-start
  142.4 0.9 copy-start.1
